TPU v7x, 32 devices: a whole 2x2x4 slice. The times are simulated.
32 devices in a mesh: groups: 2 (over y), vocab: 4 (over z), edit: 2 (over x), tok: 2 (over core).
Axes of the slice: x: 2, y: 2, z: 4, core: 2. Of those that a mesh axis runs over, the one named last changes fastest.
Arguments:
- token_ids: int32 [256], P(('groups', 'tok')), parts along dimension 0, may hold values from 0 to 4095
- valid_mask: int32 [256], P(('groups', 'tok')), parts along dimension 0, may hold values 0 or 1
- key_index: int32 [4], P('groups'), parts along dimension 0, may hold values from 0 to 3
- hidden_act: bfloat16 [256, 14336], P(('groups', 'tok'), 'vocab'), parts along dimension 0, may hold values from -6 to 6
- key_table: bfloat16 [4, 14336], P(None, 'vocab'), may hold values from -0.046875 to 0.046875
- base_out: bfloat16 [256, 4096], P(('groups', 'tok'), 'vocab'), parts along dimension 0, may hold values from -50 to 50
- value_vecs: bfloat16 [4, 4096], P(('groups', 'edit'), 'vocab'), parts along dimension 0, may hold values from -6 to 6
- norm_gain: float32 [4096], replicated, may hold values from 0.5 to 1.5
- head: bfloat16 [4096, 4096], P(('vocab', 'edit')), may hold values from -46 to 46
Outputs:
- grad_value: float32 [4, 4096], P(('groups', 'edit'), 'vocab'), parts along dimension 0
- token_kl: float32 [4, 128], P(('groups', 'edit'), 'tok'), parts along dimension 0
- target_logprob: float32 [4, 128], P(('groups', 'edit'), 'tok'), parts along dimension 0
There are 2 independent parts, one for each index of `groups`. A program takes and returns all parts, laid end to end along the dimension named above; an argument that names none is the same for every part. Nothing has to cross between parts.
All inputs are finite; a program needn't handle non-finite values. No bound on the sum of `valid_mask` on one device may be relied on, other than what follows from the above.
Results may differ from a plain program's by a relative error of at most 0.0061.
Values may be sent and summed in bfloat16 or wider, within the bound.
A program may use at most 64 MiB of HBM per device.

v0:
```python
import jax
import jax.numpy as jnp
from jax import lax
from jax.sharding import PartitionSpec as P

NORM_EPS = 1e-05


def rms_scale(hidden_rows):
    return lax.rsqrt(jnp.mean(hidden_rows * hidden_rows, axis=-1, keepdims=True) + NORM_EPS)


def per_device(
    token_ids, valid_mask, key_index, hidden_act, key_table, base_out, value_vecs, norm_gain, head
):
    vocab_rows = head.shape[0]
    edit_rows = value_vecs.shape[0]
    piece_width = value_vecs.shape[1]
    key_slots = jnp.arange(key_table.shape[0], dtype=jnp.int32)
    select = (key_index[:, None] == key_slots[None, :]).astype(jnp.bfloat16)
    edit_keys = jnp.dot(select, key_table, preferred_element_type=jnp.float32).astype(jnp.bfloat16)
    coeff_part = lax.dot_general(
        edit_keys, hidden_act, (((1,), (1,)), ((), ())), preferred_element_type=jnp.float32
    )
    coeff = lax.psum(coeff_part, "vocab")
    base_rows, local_values = (
        lax.all_gather(base_out, "vocab", axis=1, tiled=True),
        lax.all_gather(value_vecs, "vocab", axis=1, tiled=True),
    )
    values = lax.all_gather(local_values, "edit", axis=0, tiled=True)
    base32 = base_rows.astype(jnp.float32)
    base_norm = (norm_gain * base32 * rms_scale(base32)).astype(jnp.bfloat16)
    base_logits = lax.dot_general(
        base_norm, head, (((1,), (1,)), ((), ())), preferred_element_type=jnp.float32
    )
    edited = base32[None, :, :] + coeff[:, :, None] * values.astype(jnp.float32)[:, None, :]
    row_scale = rms_scale(edited)
    normed = (norm_gain * edited * row_scale).astype(jnp.bfloat16)
    logits = jnp.einsum("etd,vd->etv", normed, head, preferred_element_type=jnp.float32)
    vocab_start = lax.axis_index(("vocab", "edit")) * vocab_rows
    vocab_ids = vocab_start + jnp.arange(vocab_rows, dtype=jnp.int32)
    onehot = (token_ids[:, None] == vocab_ids[None, :]).astype(jnp.float32)
    peak_base = jnp.max(base_logits, axis=-1)
    peak_edit = jnp.max(logits, axis=-1)
    peak_base, peak_edit = lax.pmax((peak_base, peak_edit), ("vocab", "edit"))
    base_exp = jnp.exp(base_logits - peak_base[:, None])
    base_total = jnp.sum(base_exp, axis=-1)
    edit_total = jnp.sum(jnp.exp(logits - peak_edit[:, :, None]), axis=-1)
    cross_sum = jnp.sum(base_exp[None, :, :] * (base_logits[None, :, :] - logits), axis=-1)
    target = jnp.sum(onehot[None, :, :] * logits, axis=-1)
    base_total, edit_total, cross_sum, target = lax.psum(
        (base_total, edit_total, cross_sum, target), ("vocab", "edit")
    )
    base_lse = peak_base + jnp.log(base_total)
    edit_lse = peak_edit + jnp.log(edit_total)
    valid = valid_mask.astype(jnp.float32)
    token_kl = valid[None, :] * (cross_sum / base_total[None, :] - base_lse[None, :] + edit_lse)
    target_logprob = target - edit_lse
    base_prob = jnp.exp(base_logits - base_lse[:, None])
    edit_prob = jnp.exp(logits - edit_lse[:, :, None])
    logit_grad = (valid[None, :, None] * (edit_prob - base_prob[None, :, :])).astype(jnp.bfloat16)
    back_rows = jnp.einsum("etv,vd->etd", logit_grad, head, preferred_element_type=jnp.float32)
    grad_y = norm_gain * back_rows
    grad_o = row_scale * grad_y - edited * row_scale**3 * jnp.mean(
        grad_y * edited, axis=-1, keepdims=True
    )
    grad_part = jnp.sum(coeff[:, :, None] * grad_o, axis=1)
    edit_start = lax.axis_index("edit") * edit_rows
    grad_total = lax.psum(grad_part, ("vocab", "edit", "tok"))
    grad_mine = lax.dynamic_slice_in_dim(grad_total, edit_start, edit_rows, 0)
    grad_piece = lax.dynamic_slice_in_dim(
        grad_mine, lax.axis_index("vocab") * piece_width, piece_width, 1
    )
    kl_mine = lax.dynamic_slice_in_dim(token_kl, edit_start, edit_rows, 0)
    target_mine = lax.dynamic_slice_in_dim(target_logprob, edit_start, edit_rows, 0)
    return (grad_piece, kl_mine, target_mine)


def solution(mesh):
    placed = (
        P(("groups", "tok")),
        P(("groups", "tok")),
        P("groups"),
        P(("groups", "tok"), "vocab"),
        P(None, "vocab"),
        P(("groups", "tok"), "vocab"),
        P(("groups", "edit"), "vocab"),
        P(),
        P(("vocab", "edit"), None),
    )
    return jax.shard_map(
        per_device,
        mesh=mesh,
        in_specs=placed,
        out_specs=(
            P(("groups", "edit"), "vocab"),
            P(("groups", "edit"), "tok"),
            P(("groups", "edit"), "tok"),
        ),
        check_vma=False,
    )
```

profile of v0, /device:TPU:0, one launch (start us, length us, event | category | flops | bytes accessed | tf_op | source)
XLA Modules:
  0.0 156.0 jit_solution(18408327459742363050)
XLA Ops:
  0.6 0.0 copy-start
  0.7 0.7 convert_element_type.32
  1.4 0.3 copy-done
  1.7 1.1 fusion.3
  2.8 13.4 %psum.42 = f32[2,64]{1,0:T(2,128)S(1)} all-reduce(f32[2,64]{1,0:T(2,128)S(1)} %fusion.3), channel_id=1, replica_groups=mesh['groups'=2,'vocab'=4,'edit'=2,'tok'=2] {'vocab'}, use_global_device_ids=true, to_apply=%region_0.0 | all-reduce | flops 128 | bytes 1024 | tf_op jit(solution)/shard_map/psum | solution.py:25
  16.3 13.3 %all_gather.10 = bf16[1,4096]{1,0:T(2,128)(2,1)S(1)} all-gather(bf16[1,1024]{1,0:T(2,128)(2,1)} %param.15), channel_id=1, replica_groups=mesh['groups'=2,'vocab'=4,'edit'=2,'tok'=2] {'vocab'}, dimensions={1}, use_global_device_ids=true | all-gather | bytes 10240 | tf_op jit(solution)/shard_map/all_gather | solution.py:28
  29.5 4.4 %all-gather = bf16[2,1,4096]{2,1,0:T(2,128)(2,1)S(1)} all-gather(bf16[1,1,4096]{2,1,0:T(2,128)(2,1)S(1)} %bitcast.20), channel_id=1, replica_groups=mesh['groups'=2,'vocab'=4,'edit'=2,'tok'=2] {'edit'}, dimensions={0}, use_global_device_ids=true | all-gather | bytes 24576 | tf_op jit(solution)/shard_map/all_gather | solution.py:30
  34.0 0.7 compare_convert_fusion
  34.7 15.0 %all_gather.9 = bf16[64,4096]{1,0:T(8,128)(2,1)S(1)} all-gather(bf16[64,1024]{1,0:T(8,128)(2,1)} %param.14), channel_id=1, replica_groups=mesh['groups'=2,'vocab'=4,'edit'=2,'tok'=2] {'vocab'}, dimensions={1}, use_global_device_ids=true | all-gather | bytes 655360 | tf_op jit(solution)/shard_map/all_gather | solution.py:27
  49.7 0.2 multiply_reduce_fusion.3
  49.9 0.0 copy-start.1
  49.9 3.9 %fusion.24 = (f32[64]{0:T(128)S(1)}, f32[64,512]{1,0:T(8,128)S(1)}) fusion(bf16[512,4096]{1,0:T(8,128)(2,1)} %param.17, f32[64]{0:T(128)S(1)} %add_rsqrt_fusion.1, f32[4096]{0:T(1024)} %param.16, bf16[64,4096]{1,0:T(8,128)(2,1)S(1)} %all_gather.9), kind=kOutput, calls=%fused_computation.48 | convolution fusion | flops 269516736 | bytes 4866560 | tf_op jit(solution)/shard_map/dot_general | solution.py:33
  53.8 0.0 copy-start.2
  53.8 0.1 convert_element_type.30
  53.9 0.4 multiply_reduce_fusion.2
  54.3 0.0 copy-done.1
  54.3 0.2 copy-done.2
  54.5 1.6 %fusion.25 = (f32[2,64]{1,0:T(2,128)S(1)}, f32[2,64,512]{2,1,0:T(8,128)S(1)}) fusion(bf16[512,4096]{1,0:T(8,128)(2,1)S(1)} %copy-done.1, f32[4096]{0:T(1024)S(1)} %copy-done.2, f32[2,64]{1,0:T(2,128)S(1)} %get-tuple-element.17, f32[2,4096]{1,0:T(2,128)S(1)} %bitcast.17, f32[64,4096]{1,0:T(8,128)S(1)} %convert_element_type.30, f32[2,64]{1,0:T(2,128)S(1)} %psum.42), kind=kOutput, calls=%fused_computation.49 | convolution fusion | flops 539557760 | bytes 5555712 | tf_op jit(solution)/shard_map/etd,vd->etv/dot_general | solution.py:39
  56.1 18.6 %all-reduce.1 = (f32[64]{0:T(128)S(1)}, f32[2,64]{1,0:T(2,128)S(1)}) all-reduce(f32[64]{0:T(128)S(1)} %get-tuple-element.18, f32[2,64]{1,0:T(2,128)S(1)} %get-tuple-element.20), channel_id=1, replica_groups=mesh['groups'=2,'vocab'=4,'edit'=2,'tok'=2] {'vocab','edit'}, use_global_device_ids=true, to_apply=%region_8.0 | all-reduce | flops 192 | bytes 1536 | tf_op jit(solution)/shard_map/pmax | solution.py:45
  74.7 0.2 fusion.23
  74.9 0.2 multiply_reduce_fusion.4
  75.1 17.7 %all-reduce = (f32[64]{0:T(128)S(1)}, f32[2,64]{1,0:T(2,128)S(1)}, f32[2,64]{1,0:T(2,128)S(1)}, f32[2,64]{1,0:T(2,128)S(1)}) all-reduce(f32[64]{0:T(128)S(1)} %get-tuple-element.14, f32[2,64]{1,0:T(2,128)S(1)} %get-tuple-element.5, ...), channel_id=1, replica_groups=mesh['groups'=2,'vocab'=4,'edit'=2,'tok'=2] {'vocab','edit'}, use_global_device_ids=true, to_apply=%region_10.0 | all-reduce | flops 448 | bytes 3584 | tf_op jit(solution)/shard_map/psum | solution.py:51
  92.8 0.1 subtract_exponential_fusion
  92.9 0.5 constant_dynamic-slice_fusion
  93.4 3.4 %multiply_reduce_fusion.1 = (f32[2,64]{1,0:T(2,128)S(1)}, f32[2,64,4096]{2,1,0:T(8,128)S(1)}) fusion(f32[2,4096]{1,0:T(2,128)S(1)} %bitcast.18, f32[64,4096]{1,0:T(8,128)S(1)} %convert_element_type.30, f32[2,64]{1,0:T(2,128)S(1)} %psum.42, bf16[512,4096]{1,0:T(8,128)(2,1)} %param.17, f32[2,64,512]{2,1,0:T(8,128)S(1)} %get-tuple-element.21, ...), kind=kOutput, calls=%fused_computation.6 | convolution fusion | flops 539754368 | bytes 7784192 | tf_op jit(solution)/shard_map/etv,vd->etd/dot_general | solution.py:62
  96.9 0.8 multiply_reduce_fusion
  97.7 57.6 %psum.45 = f32[2,4096]{1,0:T(2,128)S(1)} all-reduce(f32[2,4096]{1,0:T(2,128)S(1)} %multiply_reduce_fusion), channel_id=1, replica_groups=mesh['groups'=2,'vocab'=4,'edit'=2,'tok'=2] {'vocab','edit','tok'}, use_global_device_ids=true, to_apply=%region_13.0 | all-reduce | flops 8192 | bytes 65536 | tf_op jit(solution)/shard_map/psum | solution.py:69
  155.3 0.7 dynamic_slice.10
  (8 shorter events, 0.1 us)
Async XLA Ops:
  0.6 1.0 copy-start
  49.9 4.4 %copy-start.1 = (bf16[512,4096]{1,0:T(8,128)(2,1)S(1)}, bf16[512,4096]{1,0:T(8,128)(2,1)}, u32[]{:S(2)}) copy-start(bf16[512,4096]{1,0:T(8,128)(2,1)} %param.17) | copy-start | bytes 12582916
  53.8 0.7 copy-start.2
where the time goes:
time: 156 us
  blocking collectives  140 us (90%)
  matrix products  10 us (6%)
  other arithmetic  3.51 us (2%)
  local copies, waits for them, and re-layouts  1.73 us (1%)
    psum x1, blocking collectives, per_device(): grad_total = lax.psum(grad_part, ('vocab', 'edit', 'tok'))  57.6 us
    pmax x1, blocking collectives, per_device(): peak_base, peak_edit = lax.pmax((peak_base, peak_edit), ('vocab', 'edit'))  18.6 us
    psum x1, blocking collectives, per_device(): lax.psum((base_total, edit_total, cross_sum, target), ('vocab', 'edit'))  17.7 us
    all_gather x1, blocking collectives, per_device(): lax.all_gather(base_out, 'vocab', axis=1, tiled=True)  15 us
    psum x1, blocking collectives, per_device(): coeff = lax.psum(coeff_part, 'vocab')  13.4 us
    all_gather x1, blocking collectives, per_device(): lax.all_gather(value_vecs, 'vocab', axis=1, tiled=True)  13.3 us
    all_gather x1, blocking collectives, per_device(): values = lax.all_gather(local_values, 'edit', axis=0, tiled=True)  4.4 us
    dot_general x1, matrix products, per_device(): lax.dot_general(base_norm, head, (((1,), (1,)), ((), ())), preferred_elem...  3.87 us

commit v1 on v0

--- a/solution.py
+++ b/solution.py
@@ -22,7 +22,9 @@
     coeff_part = lax.dot_general(
         edit_keys, hidden_act, (((1,), (1,)), ((), ())), preferred_element_type=jnp.float32
     )
-    coeff = lax.psum(coeff_part, "vocab")
+    coeff = coeff_part
+    for hop in (1, 2):
+        coeff = coeff + lax.ppermute(coeff, "vocab", [(dev, dev ^ hop) for dev in range(4)])
     base_rows, local_values = (
         lax.all_gather(base_out, "vocab", axis=1, tiled=True),
         lax.all_gather(value_vecs, "vocab", axis=1, tiled=True),

time: 156 us -> 154 us (0.987)
  blocking collectives: 140 us -> 128 us
  starting transfers between devices: 0 us -> 3.85 us
  waiting for transfers between devices: 0 us -> 3.68 us
  matrix products: 10 us -> 12.1 us
    psum x1 -> x0, blocking collectives: 13.4 us -> none  [per_device(): coeff = lax.psum(coeff_part, 'vocab')]
    ppermute x0 -> x2, starting transfers between devices: none -> 3.85 us  [per_device(): lax.ppermute(coeff, 'vocab', [(dev, dev ^ hop) for dev in range(4)])]
    ppermute x0 -> x2, waiting for transfers between devices: none -> 3.68 us  [per_device(): lax.ppermute(coeff, 'vocab', [(dev, dev ^ hop) for dev in range(4)])]
    dot_general x1, matrix products: 1.62 us -> 3.82 us  [per_device(): jnp.einsum('etd,vd->etv', normed, head, preferred_element_type=jnp.float32)]
  transfers between devices with their start and end apart: 0 -> 2, of which waited for: 0 -> 1; matrix products, arithmetic and copies ran while one was open for 0% -> 3% of each run, Pallas kernels for 0% -> 0%
where the time goes in v1:
time: 154 us
  blocking collectives  128 us (83%)
  matrix products  12.1 us (8%)
  starting transfers between devices  3.85 us (2%)
  waiting for transfers between devices  3.68 us (2%)
  other arithmetic  2.81 us (2%)
  local copies, waits for them, and re-layouts  2.25 us (1%)
    psum x1, blocking collectives, per_device(): grad_total = lax.psum(grad_part, ('vocab', 'edit', 'tok'))  57.6 us
    pmax x1, blocking collectives, per_device(): peak_base, peak_edit = lax.pmax((peak_base, peak_edit), ('vocab', 'edit'))  19.9 us
    psum x1, blocking collectives, per_device(): lax.psum((base_total, edit_total, cross_sum, target), ('vocab', 'edit'))  17.1 us
    all_gather x1, blocking collectives, per_device(): lax.all_gather(base_out, 'vocab', axis=1, tiled=True)  15.5 us
    all_gather x1, blocking collectives, per_device(): lax.all_gather(value_vecs, 'vocab', axis=1, tiled=True)  13.5 us
    all_gather x1, blocking collectives, per_device(): values = lax.all_gather(local_values, 'edit', axis=0, tiled=True)  4.55 us
    ppermute x2, starting transfers between devices, per_device(): lax.ppermute(coeff, 'vocab', [(dev, dev ^ hop) for dev in range(4)])  3.85 us
    dot_general x1, matrix products, per_device(): jnp.einsum('etd,vd->etv', normed, head, preferred_element_type=jnp.float32)  3.82 us
  transfers between devices with their start and end apart: 2, of which 1 were waited for; matrix products, arithmetic and copies ran while one was open for 3% of the time, Pallas kernels for 0%

profile of v1, /device:TPU:0, one launch (start us, length us, event | category | flops | bytes accessed | tf_op | source)
XLA Modules:
  0.0 153.6 jit_solution(5780280906328307840)
XLA Ops:
  0.6 0.0 copy-start
  0.6 1.0 copy-done
  1.7 1.1 fusion.3
  2.8 3.0 %collective-permute-start = (f32[2,64]{1,0:T(2,128)S(1)}, f32[2,64]{1,0:T(2,128)S(1)}, u32[]{:S(2)}, u32[]{:S(2)}) collective-permute-start(f32[2,64]{1,0:T(2,128)S(1)} %fusion.3), channel_id=1, source_target_pairs={{0,4},{4,0},{8,12},{12,8},{1,5},{5,1},{9,13},{13,9},{2,6},{6,2},{1... | collective-permute-start | bytes 1544 | tf_op jit(solution)/shard_map/ppermute | solution.py:27
  5.9 13.5 %all_gather.10 = bf16[1,4096]{1,0:T(2,128)(2,1)S(1)} all-gather(bf16[1,1024]{1,0:T(2,128)(2,1)} %param.15), channel_id=1, replica_groups=mesh['groups'=2,'vocab'=4,'edit'=2,'tok'=2] {'vocab'}, dimensions={1}, use_global_device_ids=true | all-gather | bytes 10240 | tf_op jit(solution)/shard_map/all_gather | solution.py:30
  19.3 15.5 %all_gather.9 = bf16[64,4096]{1,0:T(8,128)(2,1)S(1)} all-gather(bf16[64,1024]{1,0:T(8,128)(2,1)} %param.14), channel_id=1, replica_groups=mesh['groups'=2,'vocab'=4,'edit'=2,'tok'=2] {'vocab'}, dimensions={1}, use_global_device_ids=true | all-gather | bytes 655360 | tf_op jit(solution)/shard_map/all_gather | solution.py:29
  34.8 0.2 multiply_reduce_fusion.3
  35.0 0.7 compare_convert_fusion
  35.7 0.0 copy-start.2
  35.8 3.7 %fusion.24 = (f32[64]{0:T(128)S(1)}, f32[64,512]{1,0:T(8,128)S(1)}) fusion(bf16[512,4096]{1,0:T(8,128)(2,1)} %param.17, f32[64]{0:T(128)S(1)} %add_rsqrt_fusion.1, f32[4096]{0:T(1024)} %param.16, bf16[64,4096]{1,0:T(8,128)(2,1)S(1)} %all_gather.9), kind=kOutput, calls=%fused_computation.48 | convolution fusion | flops 269516736 | bytes 4866560 | tf_op jit(solution)/shard_map/dot_general | solution.py:35
  39.5 0.0 copy-start.1
  39.5 4.5 %all-gather = bf16[2,1,4096]{2,1,0:T(2,128)(2,1)S(1)} all-gather(bf16[1,1,4096]{2,1,0:T(2,128)(2,1)S(1)} %bitcast.20), channel_id=1, replica_groups=mesh['groups'=2,'vocab'=4,'edit'=2,'tok'=2] {'edit'}, dimensions={0}, use_global_device_ids=true | all-gather | bytes 24576 | tf_op jit(solution)/shard_map/all_gather | solution.py:32
  44.0 0.1 convert_element_type.30
  44.1 0.0 collective-permute-done
  44.1 0.8 collective-permute-start.1
  44.9 0.0 copy-done.2
  45.0 3.7 %collective-permute-done.1 = f32[2,64]{1,0:T(2,128)S(1)} collective-permute-done((f32[2,64]{1,0:T(2,128)S(1)}, f32[2,64]{1,0:T(2,128)S(1)}, u32[]{:S(2)}, u32[]{:S(2)}) %collective-permute-start.1) | collective-permute-done | bytes 544 | tf_op jit(solution)/shard_map/ppermute | solution.py:27
  48.7 0.4 multiply_reduce_fusion.2
  49.1 0.0 copy-done.1
  49.1 3.8 %fusion.25 = (f32[2,64]{1,0:T(2,128)S(1)}, f32[2,64,512]{2,1,0:T(8,128)S(1)}) fusion(bf16[512,4096]{1,0:T(8,128)(2,1)} %param.17, f32[4096]{0:T(1024)S(1)} %copy-done.1, f32[2,64]{1,0:T(2,128)S(1)} %get-tuple-element.17, f32[2,4096]{1,0:T(2,128)S(1)} %bitcast.17, f32[64,4096]{1,0:T(8,128)S(1)} %convert_element_type.30, f32[2,64]{1,0:T(2,128)S(1)} %add.82), kind=kOutput, calls=%fused_computation.49 | convolution fusion | flops 539557760 | bytes 5555712 | tf_op jit(solution)/shard_map/etd,vd->etv/dot_general | solution.py:41
  53.0 19.9 %all-reduce.1 = (f32[64]{0:T(128)S(1)}, f32[2,64]{1,0:T(2,128)S(1)}) all-reduce(f32[64]{0:T(128)S(1)} %get-tuple-element.18, f32[2,64]{1,0:T(2,128)S(1)} %get-tuple-element.20), channel_id=1, replica_groups=mesh['groups'=2,'vocab'=4,'edit'=2,'tok'=2] {'vocab','edit'}, use_global_device_ids=true, to_apply=%region_7.0 | all-reduce | flops 192 | bytes 1536 | tf_op jit(solution)/shard_map/pmax | solution.py:47
  72.9 0.2 fusion.23
  73.1 0.2 multiply_reduce_fusion.4
  73.3 17.1 %all-reduce = (f32[64]{0:T(128)S(1)}, f32[2,64]{1,0:T(2,128)S(1)}, f32[2,64]{1,0:T(2,128)S(1)}, f32[2,64]{1,0:T(2,128)S(1)}) all-reduce(f32[64]{0:T(128)S(1)} %get-tuple-element.14, f32[2,64]{1,0:T(2,128)S(1)} %get-tuple-element.5, ...), channel_id=1, replica_groups=mesh['groups'=2,'vocab'=4,'edit'=2,'tok'=2] {'vocab','edit'}, use_global_device_ids=true, to_apply=%region_9.0 | all-reduce | flops 448 | bytes 3584 | tf_op jit(solution)/shard_map/psum | solution.py:53
  90.4 0.1 subtract_exponential_fusion
  90.6 3.4 %multiply_reduce_fusion.1 = (f32[2,64]{1,0:T(2,128)S(1)}, f32[2,64,4096]{2,1,0:T(8,128)S(1)}) fusion(f32[2,4096]{1,0:T(2,128)S(1)} %bitcast.18, f32[64,4096]{1,0:T(8,128)S(1)} %convert_element_type.30, f32[2,64]{1,0:T(2,128)S(1)} %add.82, bf16[512,4096]{1,0:T(8,128)(2,1)} %param.17, f32[2,64,512]{2,1,0:T(8,128)S(1)} %get-tuple-element.21, ...), kind=kOutput, calls=%fused_computation.6 | convolution fusion | flops 539754368 | bytes 7784192 | tf_op jit(solution)/shard_map/etv,vd->etd/dot_general | solution.py:64
  94.0 0.8 multiply_reduce_fusion
  94.8 57.6 %psum.37 = f32[2,4096]{1,0:T(2,128)S(1)} all-reduce(f32[2,4096]{1,0:T(2,128)S(1)} %multiply_reduce_fusion), channel_id=1, replica_groups=mesh['groups'=2,'vocab'=4,'edit'=2,'tok'=2] {'vocab','edit','tok'}, use_global_device_ids=true, to_apply=%region_12.0 | all-reduce | flops 8192 | bytes 65536 | tf_op jit(solution)/shard_map/psum | solution.py:71
  152.4 0.5 constant_dynamic-slice_fusion
  152.9 0.7 dynamic_slice.10
  (11 shorter events, 0.1 us)
Async XLA Ops:
  0.6 1.0 copy-start
  2.8 41.3 %collective-permute-start = (f32[2,64]{1,0:T(2,128)S(1)}, f32[2,64]{1,0:T(2,128)S(1)}, u32[]{:S(2)}, u32[]{:S(2)}) collective-permute-start(f32[2,64]{1,0:T(2,128)S(1)} %fusion.3), channel_id=1, source_target_pairs={{0,4},{4,0},{8,12},{12,8},{1,5},{5,1},{9,13},{13,9},{2,6},{6,2},{1... | collective-permute-start | bytes 1544 | tf_op jit(solution)/shard_map/ppermute | solution.py:27
  35.7 9.2 %copy-start.2 = (s32[64]{0:T(128)S(1)}, s32[64]{0:T(128)}, u32[]{:S(2)}) copy-start(s32[64]{0:T(128)} %param.10) | copy-start | bytes 772
  39.5 9.7 %copy-start.1 = (f32[4096]{0:T(1024)S(1)}, f32[4096]{0:T(1024)}, u32[]{:S(2)}) copy-start(f32[4096]{0:T(1024)} %param.16) | copy-start | bytes 49156
  44.1 4.5 %collective-permute-start.1 = (f32[2,64]{1,0:T(2,128)S(1)}, f32[2,64]{1,0:T(2,128)S(1)}, u32[]{:S(2)}, u32[]{:S(2)}) collective-permute-start(f32[2,64]{1,0:T(2,128)S(1)} %add.81), channel_id=1, source_target_pairs={{0,8},{4,12},{8,0},{12,4},{1,9},{5,13},{9,1},{13,5},{2,10},{6,14},... | collective-permute-start | bytes 1544 | tf_op jit(solution)/shard_map/ppermute | solution.py:27
